TPU v7x, 32 devices: a whole 2x2x4 slice. The times are simulated.
32 devices in a mesh: row: 8 (over z, y), col: 4 (over x, core).
Axes of the slice: x: 2, y: 2, z: 4, core: 2. Of those that a mesh axis runs over, the one named last changes fastest.
Arguments:
- left_blocks: bfloat16 [2, 128, 512, 128], P(None, 'row', 'col'), may hold values from -0.1875 to 0.1875
- right_blocks: bfloat16 [128, 512, 128], P('row', 'col'), may hold values from -6 to 6
- left_index: int32 [2, 512, 32], P(None, 'row', 'col'), may hold values from 0 to 16, as said below
- right_index: int32 [2, 512, 32], P(None, 'row', 'col'), may hold values from 0 to 15
Outputs:
- out_blocks: bfloat16 [512, 512, 128], P('row', 'col')
Inputs may be any that keep to these rules, and one draw needn't show every extreme that they name: `left_index`: the value 16 marks a padded pair that adds nothing; in every step and on every device each result block has 1 to 8 live pairs.
All inputs are finite; a program needn't handle non-finite values.
Results may differ from a plain program's by a relative error of at most 0.001.
Values may be sent and summed in bfloat16 or wider, within the bound.
No kernel may reach another device: no remote copies, remote signals or barrier semaphores. Data moves between devices by JAX's collectives and lax.ppermute only.
A program may use at most 128 MiB of HBM per device.

v0:
```python
import jax
import jax.numpy as jnp
from jax import lax
from jax.sharding import PartitionSpec as P


def from_root(value, axis, source):
    kept = jnp.where(lax.axis_index(axis) == source, value, 0).astype(value.dtype)
    return lax.psum(kept, axis)


def shifted(x, axis, by):
    size = lax.axis_size(axis)
    return lax.ppermute(x, axis, [(i, (i + by) % size) for i in range(size)])


def fetch_left(left_blocks, step_index, row_at, row_count, col_count):
    panel_index = (row_at + step_index) % row_count
    own_slot = panel_index // col_count
    root_col = panel_index % col_count
    own_panel = lax.dynamic_index_in_dim(left_blocks, own_slot, 0, keepdims=False)
    fetched = from_root(own_panel, "col", root_col)
    return fetched


def grouped(left_panel, right_panel, left_rows, right_rows):
    block_size = left_panel.shape[-1]
    padded = jnp.concatenate(
        [left_panel, jnp.zeros((1, block_size, block_size), left_panel.dtype)], axis=0
    )
    slot_count, group_size = left_rows.shape
    bundle_size = min(slot_count, 32)

    def one_bundle(indices):
        left_tiles = jnp.take(padded, indices[0], axis=0)
        right_tiles = jnp.take(right_panel, indices[1], axis=0)
        return jnp.einsum(
            "sgij,sgjl->sil", left_tiles, right_tiles, preferred_element_type=jnp.float32
        )

    bundled = (
        left_rows.reshape(slot_count // bundle_size, bundle_size, group_size),
        right_rows.reshape(slot_count // bundle_size, bundle_size, group_size),
    )
    result = lax.map(one_bundle, bundled)
    return result.reshape(slot_count, block_size, block_size)


def per_device(left_blocks, right_blocks, left_index, right_index):
    row_count = lax.axis_size("row")
    col_count = lax.axis_size("col")
    row_at = lax.axis_index("row")
    step_count = left_index.shape[0]
    accumulated = None
    right_panel = right_blocks
    for step_index in range(step_count):
        if step_index > 0:
            right_panel = shifted(right_panel, "row", -1)
        left_panel = fetch_left(left_blocks, step_index, row_at, row_count, col_count)
        contribution = grouped(
            left_panel, right_panel, left_index[step_index], right_index[step_index]
        )
        accumulated = contribution if accumulated is None else accumulated + contribution
    return accumulated.astype(jnp.bfloat16)


def solution(mesh):
    return jax.shard_map(
        per_device,
        mesh=mesh,
        in_specs=(
            P(None, "row", "col", None),
            P("row", "col", None),
            P(None, "row", "col"),
            P(None, "row", "col"),
        ),
        out_specs=P("row", "col", None),
        check_vma=False,
    )
```

profile of v0, /device:TPU:0, one launch (start us, length us, event | category | flops | bytes accessed | tf_op | source)
XLA Modules:
  0.0 170.9 jit_solution(15086971149026818629)
XLA Ops:
  6.5 0.0 all-reduce.5.cloned.1.call-start
  6.5 2.2 %select_bitcast_fusion = (bf16[16,128,128]{2,1,0:T(8,128)(2,1)}, bf16[16,128,128]{2,1,0:T(8,128)(2,1)}) fusion(bf16[2,16,128,128]{3,2,1,0:T(8,128)(2,1)} %param.12, s32[]{:T(128)S(6)} %select_n.77, pred[]{:T(512)S(6)} %eq.12, s32[]{:T(128)S(6)} %select_n.70, pred[]{:T(512)S(6)} %eq.11), kind=kLoop, calls=%fused_computation.33 | loop fusion | flops 524288 | bytes 2097162 | tf_op jit(solution)/shard_map/jit(_where)/select_n | solution.py:8
  8.8 0.0 all-reduce.5.cloned.1.call-update
  8.8 6.1 %collective-permute-start = (bf16[16,128,128]{2,1,0:T(8,128)(2,1)}, bf16[16,128,128]{2,1,0:T(8,128)(2,1)S(1)}, u32[]{:S(2)}, u32[]{:S(2)}) collective-permute-start(bf16[16,128,128]{2,1,0:T(8,128)(2,1)} %param.13), channel_id=1, source_target_pairs={{0,28},{4,0},{8,4},{12,8},{16,12},{20,16},{24,20},{28,24},{1,29},{... | collective-permute-start | bytes 1572872 | tf_op jit(solution)/shard_map/ppermute | solution.py:14
  14.9 0.7 fusion.23
  15.6 0.1 copy.11
  15.7 0.7 fusion.22
  16.4 0.1 copy.12
  16.5 0.1 copy.9
  16.6 0.1 copy.10
  16.6 32.1 %all-reduce.5.cloned.1.call-done = (bf16[16,128,128]{2,1,0:T(8,128)(2,1)}, bf16[16,128,128]{2,1,0:T(8,128)(2,1)}) async-done(((bf16[16,128,128]{2,1,0:T(8,128)(2,1)}, bf16[16,128,128]{2,1,0:T(8,128)(2,1)}), (bf16[16,128,128]{2,1,0:T(8,128)(2,1)}, bf16[16,128,128]{2,1,0:T(8,128)(2,1)})) %all-reduce.5.cloned.1.call-update) | async-done | bytes 1048592 | tf_op jit(solution)/shard_map/psum | solution.py:9
  48.8 1.1 concatenate.7
  49.9 0.0 collective-permute-done
  49.9 2.5 %broadcast.27.clone.1 = f32[2,32,128,128]{3,2,1,0:T(8,128)} broadcast(f32[]{:T(128)} %constant.99.clone.1), dimensions={} | broadcast | bytes 4194308 | tf_op jit(solution)/shard_map/broadcast.2
  52.3 0.0 copy-start.1
  52.3 0.0 copy-start
  52.3 51.7 %while.21 = (s32[]{:T(128)}, f32[2,32,128,128]{3,2,1,0:T(8,128)}, s32[2,32,8]{2,1,0:T(8,128)S(1)}, bf16[17,128,128]{2,1,0:T(8,128)(2,1)S(1)}, s32[2,32,8]{2,1,0:...) while((s32[]{:T(128)}, f32[2,32,128,128]{3,2,1,0:T(8,128)}, s32[2,32,8]{2,1,0:T(8,128)S(1)}, ...), condition=%wide.region_5.8_spmd, body=%wide.region_4.7_spmd.sunk | while | flops 1082135552 | bytes 52450896 | solution.py:45
  52.4 0.1 reshape.100
  52.5 8.6 %gather_fusion.2 = bf16[256,128,128]{2,1,0:T(8,128)(2,1)} fusion(bf16[16,128,128]{2,1,0:T(8,128)(2,1)S(1)} %get-tuple-element.247, s32[1024]{0:T(1024)S(1)} %pad_clamp_fusion.10), kind=kCustom, calls=%fused_computation.3.clone.clone.1 | custom fusion | bytes 16778240 | tf_op jit(solution)/shard_map/while/body/eval_jaxpr/jit(_take)/gather | solution.py:36
  61.0 0.1 reshape.101
  61.1 8.5 %gather_fusion.3 = bf16[256,128,128]{2,1,0:T(8,128)(2,1)} fusion(bf16[17,128,128]{2,1,0:T(8,128)(2,1)S(1)} %get-tuple-element.245, s32[1024]{0:T(1024)S(1)} %pad_clamp_fusion.11), kind=kCustom, calls=%fused_computation.2.clone.clone.1 | custom fusion | bytes 16778240 | tf_op jit(solution)/shard_map/while/body/eval_jaxpr/jit(_take)/gather | solution.py:35
  69.6 8.6 %bitcast_dynamic-update-slice_fusion.5 = f32[2,32,128,128]{3,2,1,0:T(8,128)} fusion(f32[2,32,128,128]{3,2,1,0:T(8,128)} %get-tuple-element.236, s32[]{:T(128)} %get-tuple-element.235, bf16[32,8,128,128]{3,2,1,0:T(8,128)(2,1)} %bitcast.45, pred[32,8]{1,0:T(8,128)(4,1)S(1)} %get-tuple-element.204, bf16[32,8,128,128]{3,2,1,0:T(8,128)(2,1)} %bitcast.47, ...), kind=kOutput, calls=%fused_computation.24.clone.1 | convolution fusion | flops 1082130432 | bytes 18875392 | tf_op jit(solution)/shard_map/while/body/eval_jaxpr/sgij,sgjl->sil/dot_general | solution.py:37
  78.2 0.1 reshape.100
  78.3 8.6 %gather_fusion.2 = bf16[256,128,128]{2,1,0:T(8,128)(2,1)} fusion(bf16[16,128,128]{2,1,0:T(8,128)(2,1)S(1)} %get-tuple-element.247, s32[1024]{0:T(1024)S(1)} %pad_clamp_fusion.10), kind=kCustom, calls=%fused_computation.3.clone.clone.1 | custom fusion | bytes 16778240 | tf_op jit(solution)/shard_map/while/body/eval_jaxpr/jit(_take)/gather | solution.py:36
  86.9 0.1 reshape.101
  87.0 8.5 %gather_fusion.3 = bf16[256,128,128]{2,1,0:T(8,128)(2,1)} fusion(bf16[17,128,128]{2,1,0:T(8,128)(2,1)S(1)} %get-tuple-element.245, s32[1024]{0:T(1024)S(1)} %pad_clamp_fusion.11), kind=kCustom, calls=%fused_computation.2.clone.clone.1 | custom fusion | bytes 16778240 | tf_op jit(solution)/shard_map/while/body/eval_jaxpr/jit(_take)/gather | solution.py:35
  95.5 8.6 %bitcast_dynamic-update-slice_fusion.5 = f32[2,32,128,128]{3,2,1,0:T(8,128)} fusion(f32[2,32,128,128]{3,2,1,0:T(8,128)} %get-tuple-element.236, s32[]{:T(128)} %get-tuple-element.235, bf16[32,8,128,128]{3,2,1,0:T(8,128)(2,1)} %bitcast.45, pred[32,8]{1,0:T(8,128)(4,1)S(1)} %get-tuple-element.204, bf16[32,8,128,128]{3,2,1,0:T(8,128)(2,1)} %bitcast.47, ...), kind=kOutput, calls=%fused_computation.24.clone.1 | convolution fusion | flops 1082130432 | bytes 18875392 | tf_op jit(solution)/shard_map/while/body/eval_jaxpr/sgij,sgjl->sil/dot_general | solution.py:37
  104.0 0.0 copy-done.1
  104.1 2.5 %broadcast.27.clone = f32[2,32,128,128]{3,2,1,0:T(8,128)} broadcast(f32[]{:T(128)} %constant.99.clone.1), dimensions={} | broadcast | bytes 4194308 | tf_op jit(solution)/shard_map/broadcast.2
  106.6 0.0 copy-done
  106.6 51.8 %while.20 = (s32[]{:T(128)}, f32[2,32,128,128]{3,2,1,0:T(8,128)}, s32[2,32,8]{2,1,0:T(8,128)S(1)}, bf16[17,128,128]{2,1,0:T(8,128)(2,1)S(1)}, s32[2,32,8]{2,1,0:...) while((s32[]{:T(128)}, f32[2,32,128,128]{3,2,1,0:T(8,128)}, s32[2,32,8]{2,1,0:T(8,128)S(1)}, ...), condition=%wide.region_2.5_spmd, body=%wide.region_1.4_spmd.sunk | while | flops 1082135552 | bytes 52450896 | solution.py:45
  106.6 0.1 reshape.94
  106.7 8.6 %gather_fusion = bf16[256,128,128]{2,1,0:T(8,128)(2,1)} fusion(bf16[16,128,128]{2,1,0:T(8,128)(2,1)S(1)} %get-tuple-element.226, s32[1024]{0:T(1024)S(1)} %pad_clamp_fusion.8), kind=kCustom, calls=%fused_computation.1.clone.clone.1 | custom fusion | bytes 16778240 | tf_op jit(solution)/shard_map/while/body/eval_jaxpr/jit(_take)/gather | solution.py:36
  115.3 0.1 reshape.95
  115.4 8.5 %gather_fusion.1 = bf16[256,128,128]{2,1,0:T(8,128)(2,1)} fusion(bf16[17,128,128]{2,1,0:T(8,128)(2,1)S(1)} %get-tuple-element.224, s32[1024]{0:T(1024)S(1)} %pad_clamp_fusion.9), kind=kCustom, calls=%fused_computation.clone.clone.1 | custom fusion | bytes 16778240 | tf_op jit(solution)/shard_map/while/body/eval_jaxpr/jit(_take)/gather | solution.py:35
  123.9 8.6 %bitcast_dynamic-update-slice_fusion.4 = f32[2,32,128,128]{3,2,1,0:T(8,128)} fusion(f32[2,32,128,128]{3,2,1,0:T(8,128)} %get-tuple-element.215, s32[]{:T(128)} %get-tuple-element.214, bf16[32,8,128,128]{3,2,1,0:T(8,128)(2,1)} %bitcast.46, pred[32,8]{1,0:T(8,128)(4,1)S(1)} %get-tuple-element.194, bf16[32,8,128,128]{3,2,1,0:T(8,128)(2,1)} %bitcast.48, ...), kind=kOutput, calls=%fused_computation.10.clone.1 | convolution fusion | flops 1082130432 | bytes 18875392 | tf_op jit(solution)/shard_map/while/body/eval_jaxpr/sgij,sgjl->sil/dot_general | solution.py:37
  132.4 0.1 reshape.94
  132.5 8.6 %gather_fusion = bf16[256,128,128]{2,1,0:T(8,128)(2,1)} fusion(bf16[16,128,128]{2,1,0:T(8,128)(2,1)S(1)} %get-tuple-element.226, s32[1024]{0:T(1024)S(1)} %pad_clamp_fusion.8), kind=kCustom, calls=%fused_computation.1.clone.clone.1 | custom fusion | bytes 16778240 | tf_op jit(solution)/shard_map/while/body/eval_jaxpr/jit(_take)/gather | solution.py:36
  141.1 0.1 reshape.95
  141.2 8.5 %gather_fusion.1 = bf16[256,128,128]{2,1,0:T(8,128)(2,1)} fusion(bf16[17,128,128]{2,1,0:T(8,128)(2,1)S(1)} %get-tuple-element.224, s32[1024]{0:T(1024)S(1)} %pad_clamp_fusion.9), kind=kCustom, calls=%fused_computation.clone.clone.1 | custom fusion | bytes 16778240 | tf_op jit(solution)/shard_map/while/body/eval_jaxpr/jit(_take)/gather | solution.py:35
  149.8 8.5 %bitcast_dynamic-update-slice_fusion.4 = f32[2,32,128,128]{3,2,1,0:T(8,128)} fusion(f32[2,32,128,128]{3,2,1,0:T(8,128)} %get-tuple-element.215, s32[]{:T(128)} %get-tuple-element.214, bf16[32,8,128,128]{3,2,1,0:T(8,128)(2,1)} %bitcast.46, pred[32,8]{1,0:T(8,128)(4,1)S(1)} %get-tuple-element.194, bf16[32,8,128,128]{3,2,1,0:T(8,128)(2,1)} %bitcast.48, ...), kind=kOutput, calls=%fused_computation.10.clone.1 | convolution fusion | flops 1082130432 | bytes 18875392 | tf_op jit(solution)/shard_map/while/body/eval_jaxpr/sgij,sgjl->sil/dot_general | solution.py:37
  158.3 5.7 %add_convert_fusion = bf16[2,32,128,128]{3,2,1,0:T(8,128)(2,1)} fusion(f32[2,32,128,128]{3,2,1,0:T(8,128)} %get-tuple-element.71, f32[2,32,128,128]{3,2,1,0:T(8,128)} %get-tuple-element.72), kind=kLoop, calls=%fused_computation.32 | loop fusion | flops 2097152 | bytes 10485760 | tf_op jit(solution)/shard_map/convert_element_type | solution.py:64
  (13 shorter events, 0.2 us)
Async XLA Ops:
  6.5 42.2 %all-reduce.5.cloned.1.call-start = ((), (), s32[]{:S(2)}) async-start(), calls=%async_computation | async-start | bytes 2097152 | tf_op jit(solution)/shard_map/psum | solution.py:9
  8.8 41.1 %collective-permute-start = (bf16[16,128,128]{2,1,0:T(8,128)(2,1)}, bf16[16,128,128]{2,1,0:T(8,128)(2,1)S(1)}, u32[]{:S(2)}, u32[]{:S(2)}) collective-permute-start(bf16[16,128,128]{2,1,0:T(8,128)(2,1)} %param.13), channel_id=1, source_target_pairs={{0,28},{4,0},{8,4},{12,8},{16,12},{20,16},{24,20},{28,24},{1,29},{... | collective-permute-start | bytes 1572872 | tf_op jit(solution)/shard_map/ppermute | solution.py:14
  52.3 51.7 %copy-start.1 = (bf16[16,128,128]{2,1,0:T(8,128)(2,1)S(1)}, bf16[16,128,128]{2,1,0:T(8,128)(2,1)}, u32[]{:S(2)}) copy-start(bf16[16,128,128]{2,1,0:T(8,128)(2,1)} %get-tuple-element.97) | copy-start | bytes 1572868
  52.3 54.2 %copy-start = (bf16[16,128,128]{2,1,0:T(8,128)(2,1)S(1)}, bf16[16,128,128]{2,1,0:T(8,128)(2,1)}, u32[]{:S(2)}) copy-start(bf16[16,128,128]{2,1,0:T(8,128)(2,1)} %param.13) | copy-start | bytes 1572868
Sparse Core Ops, SparseCore 0:
  9.8 38.9 all-reduce.4
where the time goes:
time: 171 us
  local copies, waits for them, and re-layouts  76.8 us (45%)
  matrix products  34.2 us (20%)
  waiting for transfers between devices  32.1 us (19%)
  between operations  13.4 us (8%)
  other arithmetic  8.06 us (5%)
  starting transfers between devices  6.09 us (4%)
    gather x4, local copies, waits for them, and re-layouts, one_bundle(): right_tiles = jnp.take(right_panel, indices[1], axis=0)  34.3 us
    dot_general x4, matrix products, one_bundle(): jnp.einsum('sgij,sgjl->sil', left_tiles, right_tiles, preferred_element_t...  34.2 us
    gather x4, local copies, waits for them, and re-layouts, one_bundle(): left_tiles = jnp.take(padded, indices[0], axis=0)  34 us
    psum x1, waiting for transfers between devices, from_root(): return lax.psum(kept, axis)  32.1 us
    ppermute x1, starting transfers between devices, shifted(): return lax.ppermute(x, axis, [(i, (i + by) % size) for i in range(size)])  6.09 us
    convert_element_type x1, other arithmetic, per_device(): return accumulated.astype(jnp.bfloat16)  5.69 us
    another operation x2, local copies, waits for them, and re-layouts  4.94 us
  transfers between devices with their start and end apart: 2, of which 1 were waited for; matrix products, arithmetic and copies ran while one was open for 2% of the time, Pallas kernels for 0%

commit v1 on v0

--- a/solution.py
+++ b/solution.py
@@ -3,10 +3,14 @@
 from jax import lax
 from jax.sharding import PartitionSpec as P
 
+positions_trace = lambda array_in, chip_axis: jnp.sum(
+    jax.lax.all_gather(array_in, axis_name=chip_axis), axis=0
+)
+
 
 def from_root(value, axis, source):
     kept = jnp.where(lax.axis_index(axis) == source, value, 0).astype(value.dtype)
-    return lax.psum(kept, axis)
+    return positions_trace(kept, chip_axis=axis)
 
 
 def shifted(x, axis, by):

time: 171 us -> 160 us (0.936)
  waiting for transfers between devices: 32.1 us -> 17.6 us
  other arithmetic: 8.06 us -> 12.1 us
    psum x1 -> x0, waiting for transfers between devices: 32.1 us -> none  [from_root(): return lax.psum(kept, axis)]
    all_gather x0 -> x2, waiting for transfers between devices: none -> 17.6 us  [jax.lax.all_gather(array_in, axis_name=chip_axis)]
    reduce_sum x0 -> x2, other arithmetic: none -> 4.05 us  [jnp.sum(jax.lax.all_gather(array_in, axis_name=chip_axis), axis=0)]
  transfers between devices with their start and end apart: 2 -> 3, of which waited for: 1 -> 1; matrix products, arithmetic and copies ran while one was open for 2% -> 36% of each run, Pallas kernels for 0% -> 0%
where the time goes in v1:
time: 160 us
  local copies, waits for them, and re-layouts  75.9 us (47%)
  matrix products  34.3 us (21%)
  waiting for transfers between devices  17.6 us (11%)
  between operations  13.4 us (8%)
  other arithmetic  12.1 us (8%)
  starting transfers between devices  6.13 us (4%)
    gather x4, local copies, waits for them, and re-layouts, one_bundle(): right_tiles = jnp.take(right_panel, indices[1], axis=0)  34.4 us
    dot_general x4, matrix products, one_bundle(): jnp.einsum('sgij,sgjl->sil', left_tiles, right_tiles, preferred_element_t...  34.3 us
    gather x4, local copies, waits for them, and re-layouts, one_bundle(): left_tiles = jnp.take(padded, indices[0], axis=0)  34 us
    all_gather x2, waiting for transfers between devices, jax.lax.all_gather(array_in, axis_name=chip_axis)  17.6 us
    ppermute x1, starting transfers between devices, shifted(): return lax.ppermute(x, axis, [(i, (i + by) % size) for i in range(size)])  6.09 us
    convert_element_type x1, other arithmetic, per_device(): return accumulated.astype(jnp.bfloat16)  5.69 us
    another operation x2, local copies, waits for them, and re-layouts  4.95 us
    reduce_sum x2, other arithmetic, jnp.sum(jax.lax.all_gather(array_in, axis_name=chip_axis), axis=0)  4.05 us
  transfers between devices with their start and end apart: 3, of which 1 were waited for; matrix products, arithmetic and copies ran while one was open for 36% of the time, Pallas kernels for 0%

profile of v1, /device:TPU:0, one launch (start us, length us, event | category | flops | bytes accessed | tf_op | source)
XLA Modules:
  0.0 159.5 jit_solution(12808851025311508207)
XLA Ops:
  6.5 0.0 all-gather.5.cloned.1.call-start
  6.5 2.2 %dynamic-slice_select_fusion = (bf16[1,16,128,128]{3,2,1,0:T(8,128)(2,1)}, bf16[1,16,128,128]{3,2,1,0:T(8,128)(2,1)}) fusion(bf16[2,16,128,128]{3,2,1,0:T(8,128)(2,1)} %param.12, s32[]{:T(128)S(6)} %select_n.72, pred[]{:T(512)S(6)} %eq.12, s32[]{:T(128)S(6)} %select_n.66, pred[]{:T(512)S(6)} %eq.11), kind=kLoop, calls=%fused_computation.33 | loop fusion | flops 524288 | bytes 2097162 | tf_op jit(solution)/shard_map/jit(_where)/select_n | solution.py:12
  8.8 0.0 all-gather.5.cloned.1.call-update
  8.8 0.0 all-gather.3.cloned.1.call-start
  8.9 6.1 %collective-permute-start = (bf16[16,128,128]{2,1,0:T(8,128)(2,1)}, bf16[16,128,128]{2,1,0:T(8,128)(2,1)S(1)}, u32[]{:S(2)}, u32[]{:S(2)}) collective-permute-start(bf16[16,128,128]{2,1,0:T(8,128)(2,1)} %param.13), channel_id=1, source_target_pairs={{0,28},{4,0},{8,4},{12,8},{16,12},{20,16},{24,20},{28,24},{1,29},{... | collective-permute-start | bytes 1572872 | tf_op jit(solution)/shard_map/ppermute | solution.py:18
  14.9 0.0 all-gather.3.cloned.1.call-update
  15.0 0.7 fusion.23
  15.7 0.1 copy.15
  15.8 0.7 fusion.22
  16.5 0.1 copy.16
  16.5 0.1 copy.13
  16.6 0.1 copy.14
  16.7 17.5 %all-gather.5.cloned.1.call-done = bf16[4,16,128,128]{3,2,1,0:T(8,128)(2,1)} async-done(((bf16[1,16,128,128]{3,2,1,0:T(8,128)(2,1)}), bf16[4,16,128,128]{3,2,1,0:T(8,128)(2,1)}) %all-gather.5.cloned.1.call-update) | async-done | bytes 2097168 | tf_op jit(solution)/shard_map/all_gather | solution.py:7
  34.3 2.0 %reduce_sum.25 = bf16[16,128,128]{2,1,0:T(8,128)(2,1)S(1)} reduce(bf16[4,16,128,128]{3,2,1,0:T(8,128)(2,1)} %all-gather.5.cloned.1.call-done, bf16[]{:T(256)} %constant.113.clone.1), dimensions={0}, to_apply=%region_3.6 | reduce | flops 786432 | bytes 2621442 | tf_op jit(solution)/shard_map/reduce_sum | solution.py:6
  36.3 0.1 concatenate.7
  36.4 0.0 collective-permute-done
  36.4 2.5 %broadcast.24.clone.1 = f32[2,32,128,128]{3,2,1,0:T(8,128)} broadcast(f32[]{:T(128)} %constant.102.clone.1), dimensions={} | broadcast | bytes 4194308 | tf_op jit(solution)/shard_map/broadcast.2
  38.9 0.0 copy-start
  38.9 51.8 %while.21 = (s32[]{:T(128)}, f32[2,32,128,128]{3,2,1,0:T(8,128)}, s32[2,32,8]{2,1,0:T(8,128)S(1)}, bf16[17,128,128]{2,1,0:T(8,128)(2,1)S(1)}, s32[2,32,8]{2,1,0:...) while((s32[]{:T(128)}, f32[2,32,128,128]{3,2,1,0:T(8,128)}, s32[2,32,8]{2,1,0:T(8,128)S(1)}, ...), condition=%wide.region_5.8_spmd, body=%wide.region_4.7_spmd.sunk | while | flops 1082135552 | bytes 52450896 | solution.py:49
  38.9 0.1 reshape.94
  39.0 8.6 %gather_fusion.2 = bf16[256,128,128]{2,1,0:T(8,128)(2,1)} fusion(bf16[16,128,128]{2,1,0:T(8,128)(2,1)S(1)} %get-tuple-element.245, s32[1024]{0:T(1024)S(1)} %pad_clamp_fusion.10), kind=kCustom, calls=%fused_computation.3.clone.clone.1 | custom fusion | bytes 16778240 | tf_op jit(solution)/shard_map/while/body/eval_jaxpr/jit(_take)/gather | solution.py:40
  47.6 0.1 reshape.95
  47.7 8.5 %gather_fusion.3 = bf16[256,128,128]{2,1,0:T(8,128)(2,1)} fusion(bf16[17,128,128]{2,1,0:T(8,128)(2,1)S(1)} %get-tuple-element.243, s32[1024]{0:T(1024)S(1)} %pad_clamp_fusion.11), kind=kCustom, calls=%fused_computation.2.clone.clone.1 | custom fusion | bytes 16778240 | tf_op jit(solution)/shard_map/while/body/eval_jaxpr/jit(_take)/gather | solution.py:39
  56.2 8.6 %bitcast_dynamic-update-slice_fusion.5 = f32[2,32,128,128]{3,2,1,0:T(8,128)} fusion(f32[2,32,128,128]{3,2,1,0:T(8,128)} %get-tuple-element.234, s32[]{:T(128)} %get-tuple-element.233, bf16[32,8,128,128]{3,2,1,0:T(8,128)(2,1)} %bitcast.41, pred[32,8]{1,0:T(8,128)(4,1)S(1)} %get-tuple-element.202, bf16[32,8,128,128]{3,2,1,0:T(8,128)(2,1)} %bitcast.43, ...), kind=kOutput, calls=%fused_computation.24.clone.1 | convolution fusion | flops 1082130432 | bytes 18875392 | tf_op jit(solution)/shard_map/while/body/eval_jaxpr/sgij,sgjl->sil/dot_general | solution.py:41
  64.8 0.1 reshape.94
  64.9 8.6 %gather_fusion.2 = bf16[256,128,128]{2,1,0:T(8,128)(2,1)} fusion(bf16[16,128,128]{2,1,0:T(8,128)(2,1)S(1)} %get-tuple-element.245, s32[1024]{0:T(1024)S(1)} %pad_clamp_fusion.10), kind=kCustom, calls=%fused_computation.3.clone.clone.1 | custom fusion | bytes 16778240 | tf_op jit(solution)/shard_map/while/body/eval_jaxpr/jit(_take)/gather | solution.py:40
  73.5 0.1 reshape.95
  73.6 8.5 %gather_fusion.3 = bf16[256,128,128]{2,1,0:T(8,128)(2,1)} fusion(bf16[17,128,128]{2,1,0:T(8,128)(2,1)S(1)} %get-tuple-element.243, s32[1024]{0:T(1024)S(1)} %pad_clamp_fusion.11), kind=kCustom, calls=%fused_computation.2.clone.clone.1 | custom fusion | bytes 16778240 | tf_op jit(solution)/shard_map/while/body/eval_jaxpr/jit(_take)/gather | solution.py:39
  82.1 8.6 %bitcast_dynamic-update-slice_fusion.5 = f32[2,32,128,128]{3,2,1,0:T(8,128)} fusion(f32[2,32,128,128]{3,2,1,0:T(8,128)} %get-tuple-element.234, s32[]{:T(128)} %get-tuple-element.233, bf16[32,8,128,128]{3,2,1,0:T(8,128)(2,1)} %bitcast.41, pred[32,8]{1,0:T(8,128)(4,1)S(1)} %get-tuple-element.202, bf16[32,8,128,128]{3,2,1,0:T(8,128)(2,1)} %bitcast.43, ...), kind=kOutput, calls=%fused_computation.24.clone.1 | convolution fusion | flops 1082130432 | bytes 18875392 | tf_op jit(solution)/shard_map/while/body/eval_jaxpr/sgij,sgjl->sil/dot_general | solution.py:41
  90.6 0.0 all-gather.3.cloned.1.call-done
  90.6 2.0 %reduce_sum.24 = bf16[16,128,128]{2,1,0:T(8,128)(2,1)S(1)} reduce(bf16[4,16,128,128]{3,2,1,0:T(8,128)(2,1)} %all-gather.3.cloned.1.call-done, bf16[]{:T(256)} %constant.113.clone.1), dimensions={0}, to_apply=%region_0.1 | reduce | flops 786432 | bytes 2621442 | tf_op jit(solution)/shard_map/reduce_sum | solution.py:6
  92.7 0.1 concatenate.6
  92.7 2.5 %broadcast.24.clone = f32[2,32,128,128]{3,2,1,0:T(8,128)} broadcast(f32[]{:T(128)} %constant.102.clone.1), dimensions={} | broadcast | bytes 4194308 | tf_op jit(solution)/shard_map/broadcast.2
  95.2 0.0 copy-done
  95.2 51.8 %while.20 = (s32[]{:T(128)}, f32[2,32,128,128]{3,2,1,0:T(8,128)}, s32[2,32,8]{2,1,0:T(8,128)S(1)}, bf16[17,128,128]{2,1,0:T(8,128)(2,1)S(1)}, s32[2,32,8]{2,1,0:...) while((s32[]{:T(128)}, f32[2,32,128,128]{3,2,1,0:T(8,128)}, s32[2,32,8]{2,1,0:T(8,128)S(1)}, ...), condition=%wide.region_2.5_spmd, body=%wide.region_1.4_spmd.sunk | while | flops 1082135552 | bytes 52450896 | solution.py:49
  95.2 0.1 reshape.88
  95.3 8.6 %gather_fusion = bf16[256,128,128]{2,1,0:T(8,128)(2,1)} fusion(bf16[16,128,128]{2,1,0:T(8,128)(2,1)S(1)} %get-tuple-element.224, s32[1024]{0:T(1024)S(1)} %pad_clamp_fusion.8), kind=kCustom, calls=%fused_computation.1.clone.clone.1 | custom fusion | bytes 16778240 | tf_op jit(solution)/shard_map/while/body/eval_jaxpr/jit(_take)/gather | solution.py:40
  103.9 0.1 reshape.89
  104.0 8.5 %gather_fusion.1 = bf16[256,128,128]{2,1,0:T(8,128)(2,1)} fusion(bf16[17,128,128]{2,1,0:T(8,128)(2,1)S(1)} %get-tuple-element.222, s32[1024]{0:T(1024)S(1)} %pad_clamp_fusion.9), kind=kCustom, calls=%fused_computation.clone.clone.1 | custom fusion | bytes 16778240 | tf_op jit(solution)/shard_map/while/body/eval_jaxpr/jit(_take)/gather | solution.py:39
  112.5 8.6 %bitcast_dynamic-update-slice_fusion.4 = f32[2,32,128,128]{3,2,1,0:T(8,128)} fusion(f32[2,32,128,128]{3,2,1,0:T(8,128)} %get-tuple-element.213, s32[]{:T(128)} %get-tuple-element.212, bf16[32,8,128,128]{3,2,1,0:T(8,128)(2,1)} %bitcast.42, pred[32,8]{1,0:T(8,128)(4,1)S(1)} %get-tuple-element.192, bf16[32,8,128,128]{3,2,1,0:T(8,128)(2,1)} %bitcast.44, ...), kind=kOutput, calls=%fused_computation.10.clone.1 | convolution fusion | flops 1082130432 | bytes 18875392 | tf_op jit(solution)/shard_map/while/body/eval_jaxpr/sgij,sgjl->sil/dot_general | solution.py:41
  121.1 0.1 reshape.88
  121.2 8.6 %gather_fusion = bf16[256,128,128]{2,1,0:T(8,128)(2,1)} fusion(bf16[16,128,128]{2,1,0:T(8,128)(2,1)S(1)} %get-tuple-element.224, s32[1024]{0:T(1024)S(1)} %pad_clamp_fusion.8), kind=kCustom, calls=%fused_computation.1.clone.clone.1 | custom fusion | bytes 16778240 | tf_op jit(solution)/shard_map/while/body/eval_jaxpr/jit(_take)/gather | solution.py:40
  129.8 0.1 reshape.89
  129.9 8.5 %gather_fusion.1 = bf16[256,128,128]{2,1,0:T(8,128)(2,1)} fusion(bf16[17,128,128]{2,1,0:T(8,128)(2,1)S(1)} %get-tuple-element.222, s32[1024]{0:T(1024)S(1)} %pad_clamp_fusion.9), kind=kCustom, calls=%fused_computation.clone.clone.1 | custom fusion | bytes 16778240 | tf_op jit(solution)/shard_map/while/body/eval_jaxpr/jit(_take)/gather | solution.py:39
  138.4 8.5 %bitcast_dynamic-update-slice_fusion.4 = f32[2,32,128,128]{3,2,1,0:T(8,128)} fusion(f32[2,32,128,128]{3,2,1,0:T(8,128)} %get-tuple-element.213, s32[]{:T(128)} %get-tuple-element.212, bf16[32,8,128,128]{3,2,1,0:T(8,128)(2,1)} %bitcast.42, pred[32,8]{1,0:T(8,128)(4,1)S(1)} %get-tuple-element.192, bf16[32,8,128,128]{3,2,1,0:T(8,128)(2,1)} %bitcast.44, ...), kind=kOutput, calls=%fused_computation.10.clone.1 | convolution fusion | flops 1082130432 | bytes 18875392 | tf_op jit(solution)/shard_map/while/body/eval_jaxpr/sgij,sgjl->sil/dot_general | solution.py:41
  147.0 5.7 %add_convert_fusion = bf16[2,32,128,128]{3,2,1,0:T(8,128)(2,1)} fusion(f32[2,32,128,128]{3,2,1,0:T(8,128)} %get-tuple-element.71, f32[2,32,128,128]{3,2,1,0:T(8,128)} %get-tuple-element.72), kind=kLoop, calls=%fused_computation.32 | loop fusion | flops 2097152 | bytes 10485760 | tf_op jit(solution)/shard_map/convert_element_type | solution.py:68
  (12 shorter events, 0.1 us)
Async XLA Ops:
  6.5 27.7 %all-gather.5.cloned.1.call-start = ((), (), s32[]{:S(2)}) async-start(), calls=%async_computation.1 | async-start | bytes 2621440 | tf_op jit(solution)/shard_map/all_gather | solution.py:7
  8.8 81.8 %all-gather.3.cloned.1.call-start = ((), (), s32[]{:S(2)}) async-start(), calls=%async_computation | async-start | bytes 2621440 | tf_op jit(solution)/shard_map/all_gather | solution.py:7
  8.9 27.5 %collective-permute-start = (bf16[16,128,128]{2,1,0:T(8,128)(2,1)}, bf16[16,128,128]{2,1,0:T(8,128)(2,1)S(1)}, u32[]{:S(2)}, u32[]{:S(2)}) collective-permute-start(bf16[16,128,128]{2,1,0:T(8,128)(2,1)} %param.13), channel_id=1, source_target_pairs={{0,28},{4,0},{8,4},{12,8},{16,12},{20,16},{24,20},{28,24},{1,29},{... | collective-permute-start | bytes 1572872 | tf_op jit(solution)/shard_map/ppermute | solution.py:18
  38.9 56.3 %copy-start = (bf16[16,128,128]{2,1,0:T(8,128)(2,1)S(1)}, bf16[16,128,128]{2,1,0:T(8,128)(2,1)}, u32[]{:S(2)}) copy-start(bf16[16,128,128]{2,1,0:T(8,128)(2,1)} %param.13) | copy-start | bytes 1572868
Sparse Core Ops, SparseCore 0:
  8.9 25.2 all-gather.4
  35.8 22.5 all-gather.2
